TPU v7x, 32 devices: a whole 2x2x4 slice. The times are simulated.
32 devices in a mesh: row: 4 (over z), col: 8 (over y, x, core).
Axes of the slice: x: 2, y: 2, z: 4, core: 2. Of those that a mesh axis runs over, the one named last changes fastest.
Arguments:
- ancestor_pivot: float32 [8, 512, 4, 1024], P(None, 'row', None, 'col'), as said below
- child_pivot: float32 [8, 512, 4, 1024], P(None, 'row', None, 'col'), as said below
- child_panel: float32 [8, 512, 4, 1024], P(None, 'row', None, 'col'), may hold values from -0.09375 to 0.09375
- block_pattern: int32 [32, 32], replicated, may hold values 0 or 1
Outputs:
- child_inverse: float32 [8, 512, 4, 1024], P(None, 'row', None, 'col')
Inputs may be any that keep to these rules, and one draw needn't show every extreme that they name: ancestor_pivot is an exactly symmetric 4096 x 4096 matrix. child_pivot is an exactly symmetric 4096 x 4096 matrix.
All inputs are finite; a program needn't handle non-finite values.
Results may differ from a plain program's by a relative error of at most 0.00005.
Values sent between devices are 32-bit elements; how exact they have to be, the bound alone decides.
A program may use at most 128 MiB of HBM per device.

v0:
```python
import jax
import jax.numpy as jnp
from jax import lax
from jax.sharding import PartitionSpec as P


def column_term(stationary, local_rows, piece):
    shaped = piece.reshape(local_rows, piece.shape[2], piece.shape[3])
    return jnp.einsum(
        "kcl,kn->cln",
        shaped,
        stationary,
        precision=lax.Precision.HIGHEST,
        preferred_element_type=jnp.float32,
    )


def local(ancestor_pivot, child_pivot, child_panel, block_pattern):
    anc_blocks = child_panel.shape[0]
    block_size = child_panel.shape[1]
    col_blocks = child_panel.shape[2]
    anc_col_blocks = ancestor_pivot.shape[2]
    child_rows = child_pivot.shape[0]
    row_count = lax.axis_size("row")
    col_count = lax.axis_size("col")
    row_index = lax.axis_index("row")
    col_index = lax.axis_index("col")
    local_rows = anc_blocks * block_size
    local_cols = col_blocks * block_size
    blocks = block_pattern.reshape(anc_blocks, row_count, col_blocks, col_count)
    local_mask = lax.dynamic_index_in_dim(blocks, row_index, 1, keepdims=False)
    local_mask = lax.dynamic_index_in_dim(local_mask, col_index, 2, keepdims=False)
    masked = child_panel * local_mask.astype(jnp.float32)[:, None, :, None]
    masked_flat = masked.reshape(local_rows, local_cols)
    panel_all = lax.all_gather(masked, "row", axis=1, tiled=True)
    panel_split = panel_all.reshape(anc_col_blocks, col_count * block_size, local_cols)
    segment = lax.all_gather(ancestor_pivot, "col", axis=3, tiled=True)
    length = segment.shape[3]
    weights = segment.reshape(local_rows, anc_col_blocks, length)
    product = jnp.einsum(
        "kcl,cln->kn",
        weights,
        panel_split,
        precision=lax.Precision.HIGHEST,
        preferred_element_type=jnp.float32,
    )
    product_blocks = product.reshape(anc_blocks, block_size, col_blocks, block_size)
    term = column_term(
        masked_flat, local_rows, lax.all_gather(product_blocks, "col", axis=3, tiled=True)
    )
    term = term.reshape(child_rows, row_count, block_size, local_cols)
    term = jnp.transpose(term, (1, 0, 2, 3)).reshape(
        row_count * child_rows * block_size, local_cols
    )
    summed = lax.psum_scatter(term, "row", scatter_dimension=0, tiled=True)
    return child_pivot + summed.reshape(child_rows, block_size, col_blocks, block_size)


def solution(mesh):
    return jax.shard_map(
        local,
        mesh=mesh,
        in_specs=(
            P(None, "row", None, "col"),
            P(None, "row", None, "col"),
            P(None, "row", None, "col"),
            P(),
        ),
        out_specs=P(None, "row", None, "col"),
        check_vma=False,
    )
```

profile of v0, /device:TPU:0, one launch (start us, length us, event | category | flops | bytes accessed | tf_op | source)
XLA Modules:
  0.0 626.5 jit_solution(12353932388971323393)
XLA Ops:
  6.5 0.0 all-gather.4.cloned.1.call-start
  6.5 0.8 reshape.28
  7.4 0.1 constant_dynamic-slice_fusion
  7.4 0.1 copy.15
  7.6 0.1 copy.9
  7.6 3.4 broadcast_multiply_fusion
  11.0 0.0 all-gather.4.cloned.1.call-update
  11.0 0.0 all-gather.6.cloned.1.call-start
  11.1 0.7 all-gather.6.cloned.1.call-update
  11.8 0.0 all-gather.8.cloned.1.call-start
  11.8 151.7 %all-gather.4.cloned.1.call-done = f32[8,512,4,128]{3,2,1,0:T(4,128)} async-done(((f32[8,128,4,128]{3,2,1,0:T(4,128)}), f32[8,512,4,128]{3,2,1,0:T(4,128)}) %all-gather.4.cloned.1.call-update) | async-done | bytes 8388624 | tf_op jit(solution)/shard_map/all_gather | solution.py:35
  163.5 10.5 %reshape.29 = f32[4,1024,512]{2,1,0:T(8,128)} reshape(f32[8,512,4,128]{3,2,1,0:T(4,128)} %all-gather.4.cloned.1.call-done) | data formatting | bytes 16777216 | tf_op jit(solution)/shard_map/reshape | solution.py:36
  174.0 82.6 %all-gather.6.cloned.1.call-done = f32[8,128,4,1024]{3,2,1,0:T(4,128)} async-done(((f32[8,128,4,128]{3,2,1,0:T(4,128)}), f32[8,128,4,1024]{3,2,1,0:T(4,128)}) %all-gather.6.cloned.1.call-update) | async-done | bytes 16777232 | tf_op jit(solution)/shard_map/all_gather | solution.py:37
  256.6 0.0 copy-start.1
  256.6 15.3 %copy.10 = f32[8,128,4,1024]{3,1,0,2:T(8,128)S(1)} copy(f32[8,128,4,1024]{3,2,1,0:T(4,128)} %all-gather.6.cloned.1.call-done) | data formatting | bytes 33554432 | tf_op jit(solution)/shard_map/all_gather | solution.py:37
  272.0 0.0 copy-done.1
  272.0 0.0 copy-start
  272.0 54.8 %convolution_bitcast_fusion.1 = f32[64,8,8,128]{3,1,2,0:T(8,128)S(1)} fusion(f32[4,1024,512]{2,1,0:T(8,128)S(1)} %copy-done.1, f32[1024,4,1024]{2,0,1:T(8,128)S(1)} %bitcast.29), kind=kOutput, calls=%fused_computation.2 | convolution fusion | flops 25769803776 | bytes 27262976 | tf_op jit(solution)/shard_map/kcl,cln->kn/dot_general | solution.py:40
  326.9 1.8 copy.16
  328.6 0.0 all-gather.8.cloned.1.call-update
  328.7 0.0 reduce-scatter.2.cloned.1.call-start
  328.7 0.0 copy-done
  328.7 1.8 reshape.37
  330.6 0.0 copy-start.2
  330.6 88.0 %all-gather.8.cloned.1.call-done = f32[8,128,4,1024]{1,0,3,2:T(8,128)} async-done(((f32[8,128,4,128]{1,0,3,2:T(8,128)}), f32[8,128,4,1024]{1,0,3,2:T(8,128)}) %all-gather.8.cloned.1.call-update) | async-done | bytes 16777232 | tf_op jit(solution)/shard_map/all_gather | solution.py:49
  418.5 18.0 %reshape.32 = f32[1024,4,1024]{0,2,1:T(8,128)} reshape(f32[8,128,4,1024]{1,0,3,2:T(8,128)} %all-gather.8.cloned.1.call-done) | data formatting | bytes 33554432 | tf_op jit(solution)/shard_map/reshape | solution.py:8
  436.5 0.0 copy-done.2
  436.5 29.1 %convolution_bitcast_fusion = f32[4,8,128,512]{3,2,0,1:T(8,128)S(1)} fusion(f32[8,4,128,1024]{3,2,1,0:T(8,128)} %bitcast.30, f32[1024,512,1,1]{1,0,2,3:T(8,128)S(1)} %copy-done.2), kind=kOutput, calls=%fused_computation | convolution fusion | flops 25769803776 | bytes 27262976 | tf_op jit(solution)/shard_map/kcl,kn->cln/dot_general | solution.py:9
  465.6 4.2 copy.12
  469.8 0.0 reduce-scatter.2.cloned.1.call-update
  469.9 144.8 %reduce-scatter.2.cloned.1.call-done = f32[1024,512]{1,0:T(8,128)} async-done(((f32[4096,512]{1,0:T(8,128)}), f32[1024,512]{1,0:T(8,128)}) %reduce-scatter.2.cloned.1.call-update) | async-done | bytes 2097168 | tf_op jit(solution)/shard_map/reduce_scatter | solution.py:55
  614.6 1.9 reshape.35
  616.6 3.5 add.19
  (1 shorter events, 0.0 us)
Async XLA Ops:
  6.5 157.0 %all-gather.4.cloned.1.call-start = ((), (), s32[]{:S(2)}) async-start(), calls=%async_computation.1 | async-start | bytes 10485760 | tf_op jit(solution)/shard_map/all_gather | solution.py:35
  11.0 245.6 %all-gather.6.cloned.1.call-start = ((), (), s32[]{:S(2)}) async-start(), calls=%async_computation.2 | async-start | bytes 18874368 | tf_op jit(solution)/shard_map/all_gather | solution.py:37
  11.8 406.8 %all-gather.8.cloned.1.call-start = ((), (), s32[]{:S(2)}) async-start(), calls=%async_computation.3 | async-start | bytes 18874368 | tf_op jit(solution)/shard_map/all_gather | solution.py:49
  256.6 15.4 %copy-start.1 = (f32[4,1024,512]{2,1,0:T(8,128)S(1)}, f32[4,1024,512]{2,1,0:T(8,128)}, u32[]{:S(2)}) copy-start(f32[4,1024,512]{2,1,0:T(8,128)} %reshape.29) | copy-start | bytes 25165828
  272.0 56.7 %copy-start = (f32[8,128,4,128]{3,2,1,0:T(4,128)S(1)}, f32[8,128,4,128]{3,2,1,0:T(4,128)}, u32[]{:S(2)}) copy-start(f32[8,128,4,128]{3,2,1,0:T(4,128)} %broadcast_multiply_fusion) | copy-start | bytes 6291460
  328.7 286.0 %reduce-scatter.2.cloned.1.call-start = ((), (), s32[]{:S(2)}) async-start(), calls=%async_computation.4 | async-start | bytes 10485760 | tf_op jit(solution)/shard_map/reduce_scatter | solution.py:55
  330.6 106.0 %copy-start.2 = (f32[1024,512,1,1]{1,0,2,3:T(8,128)S(1)}, f32[1024,512,1,1]{1,0,2,3:T(8,128)}, u32[]{:S(2)}) copy-start(f32[1024,512,1,1]{1,0,2,3:T(8,128)} %reshape.37) | copy-start | bytes 6291460
Sparse Core Ops, SparseCore 0:
  11.1 152.3 all-gather.3
  165.4 91.1 all-gather.5
  328.8 89.7 all-gather.7
  470.0 144.6 reduce-scatter.1
where the time goes:
time: 627 us
  waiting for transfers between devices  468 us (75%)
  matrix products  83.9 us (13%)
  local copies, waits for them, and re-layouts  54.7 us (9%)
  between operations  13.2 us (2%)
  other arithmetic  6.82 us (1%)
    all_gather x1, waiting for transfers between devices, local(): panel_all = lax.all_gather(masked, 'row', axis=1, tiled=True)  152 us
    reduce_scatter x1, waiting for transfers between devices, local(): summed = lax.psum_scatter(term, 'row', scatter_dimension=0, tiled=True)  145 us
    all_gather x1, waiting for transfers between devices, local(): lax.all_gather(product_blocks, 'col', axis=3, tiled=True)  88 us
    all_gather x1, waiting for transfers between devices, local(): segment = lax.all_gather(ancestor_pivot, 'col', axis=3, tiled=True)  82.6 us
    dot_general x1, matrix products, local(): jnp.einsum('kcl,cln->kn', weights, panel_split, precision=lax.Precision.H...  54.8 us
    dot_general x1, matrix products, column_term(): jnp.einsum('kcl,kn->cln', shaped, stationary, precision=lax.Precision.HIG...  29.1 us
    reshape x1, local copies, waits for them, and re-layouts, column_term(): shaped = piece.reshape(local_rows, piece.shape[2], piece.shape[3])  18 us
    all_gather x1, local copies, waits for them, and re-layouts, local(): segment = lax.all_gather(ancestor_pivot, 'col', axis=3, tiled=True)  15.3 us
  transfers between devices with their start and end apart: 4, of which 4 were waited for; matrix products, arithmetic and copies ran while one was open for 2% of the time, Pallas kernels for 0%

commit v1 on v0

--- a/solution.py
+++ b/solution.py
@@ -2,6 +2,27 @@
 import jax.numpy as jnp
 from jax import lax
 from jax.sharding import PartitionSpec as P
+
+
+def collect(x, axis, dim):
+    size, mine, span = (lax.axis_size(axis), lax.axis_index(axis), x.shape[dim])
+    ahead = [(i, (i + 1) % size) for i in range(size)]
+    backward = [(i, (i - 1) % size) for i in range(size)]
+    filled = jnp.zeros((*x.shape[:dim], size * span, *x.shape[dim + 1 :]), x.dtype)
+    filled = lax.dynamic_update_slice_in_dim(filled, x, mine * span, axis=dim)
+    from_left = from_right = x
+    half = size // 2
+    for lap in range(1, half + 1):
+        from_left = lax.ppermute(from_left, axis, ahead)
+        filled = lax.dynamic_update_slice_in_dim(
+            filled, from_left, (mine - lap) % size * span, axis=dim
+        )
+        if lap < size - half:
+            from_right = lax.ppermute(from_right, axis, backward)
+            filled = lax.dynamic_update_slice_in_dim(
+                filled, from_right, (mine + lap) % size * span, axis=dim
+            )
+    return filled
 
 
 def column_term(stationary, local_rows, piece):
@@ -45,9 +66,7 @@
         preferred_element_type=jnp.float32,
     )
     product_blocks = product.reshape(anc_blocks, block_size, col_blocks, block_size)
-    term = column_term(
-        masked_flat, local_rows, lax.all_gather(product_blocks, "col", axis=3, tiled=True)
-    )
+    term = column_term(masked_flat, local_rows, collect(product_blocks, "col", 3))
     term = term.reshape(child_rows, row_count, block_size, local_cols)
     term = jnp.transpose(term, (1, 0, 2, 3)).reshape(
         row_count * child_rows * block_size, local_cols

time: 627 us -> 710 us (1.13)
  waiting for transfers between devices: 468 us -> 519 us
  local copies, waits for them, and re-layouts: 54.7 us -> 81.9 us
    ppermute x0 -> x7, waiting for transfers between devices: none -> 140 us  [the longest x4 140 us: collect(): from_left = lax.ppermute(from_left, axis, ahead)]
    all_gather x1 -> x0, waiting for transfers between devices: 88 us -> none  [local(): lax.all_gather(product_blocks, 'col', axis=3, tiled=True)]
    dynamic_update_slice x0 -> x8, local copies, waits for them, and re-layouts: none -> 17.8 us  [the longest x4 8.9 us: collect(): lax.dynamic_update_slice_in_dim(filled, from_left, (mine - lap) % size *...]
  transfers between devices with their start and end apart: 4 -> 10, of which waited for: 4 -> 7; matrix products, arithmetic and copies ran while one was open for 2% -> 5% of each run, Pallas kernels for 0% -> 0%
where the time goes in v1:
time: 710 us; the launch traced here: 709 us
  waiting for transfers between devices  519 us (73%)
  matrix products  83.9 us (12%)
  local copies, waits for them, and re-layouts  81.9 us (12%)
  between operations  13.2 us (2%)
    all_gather x1, waiting for transfers between devices, local(): panel_all = lax.all_gather(masked, 'row', axis=1, tiled=True)  152 us
    reduce_scatter x1, waiting for transfers between devices, local(): summed = lax.psum_scatter(term, 'row', scatter_dimension=0, tiled=True)  144 us
    ppermute x4, waiting for transfers between devices, collect(): from_left = lax.ppermute(from_left, axis, ahead)  140 us
    all_gather x1, waiting for transfers between devices, local(): segment = lax.all_gather(ancestor_pivot, 'col', axis=3, tiled=True)  82.6 us
    dot_general x1, matrix products, local(): jnp.einsum('kcl,cln->kn', weights, panel_split, precision=lax.Precision.H...  54.8 us
    dot_general x1, matrix products, column_term(): jnp.einsum('kcl,kn->cln', shaped, stationary, precision=lax.Precision.HIG...  29.1 us
    reshape x1, local copies, waits for them, and re-layouts, column_term(): shaped = piece.reshape(local_rows, piece.shape[2], piece.shape[3])  18.2 us
    all_gather x1, local copies, waits for them, and re-layouts, local(): segment = lax.all_gather(ancestor_pivot, 'col', axis=3, tiled=True)  15.3 us
  transfers between devices with their start and end apart: 10, of which 7 were waited for; matrix products, arithmetic and copies ran while one was open for 5% of the time, Pallas kernels for 0%

profile of v1, /device:TPU:0, one launch (start us, length us, event | category | flops | bytes accessed | tf_op | source)
XLA Modules:
  0.0 709.4 jit_solution(11212051598143494029)
XLA Ops:
  6.5 0.0 all-gather.3.cloned.1.call-start
  6.5 0.8 reshape.28
  7.4 0.1 constant_dynamic-slice_fusion
  7.4 0.1 copy.15
  7.6 0.1 copy.9
  7.6 3.4 broadcast_multiply_fusion
  11.0 0.0 all-gather.3.cloned.1.call-update
  11.0 0.0 all-gather.5.cloned.1.call-start
  11.1 0.7 all-gather.5.cloned.1.call-update
  11.8 0.0 reduce-scatter.2.cloned.1.call-start
  11.8 151.7 %all-gather.3.cloned.1.call-done = f32[8,512,4,128]{3,2,1,0:T(4,128)} async-done(((f32[8,128,4,128]{3,2,1,0:T(4,128)}), f32[8,512,4,128]{3,2,1,0:T(4,128)}) %all-gather.3.cloned.1.call-update) | async-done | bytes 8388624 | tf_op jit(solution)/shard_map/all_gather | solution.py:56
  163.5 10.5 %reshape.29 = f32[4,1024,512]{2,1,0:T(8,128)} reshape(f32[8,512,4,128]{3,2,1,0:T(4,128)} %all-gather.3.cloned.1.call-done) | data formatting | bytes 16777216 | tf_op jit(solution)/shard_map/reshape | solution.py:57
  174.1 82.6 %all-gather.5.cloned.1.call-done = f32[8,128,4,1024]{3,2,1,0:T(4,128)} async-done(((f32[8,128,4,128]{3,2,1,0:T(4,128)}), f32[8,128,4,1024]{3,2,1,0:T(4,128)}) %all-gather.5.cloned.1.call-update) | async-done | bytes 16777232 | tf_op jit(solution)/shard_map/all_gather | solution.py:58
  256.6 0.0 copy-start.1
  256.6 15.3 %copy.10 = f32[8,128,4,1024]{3,1,0,2:T(8,128)S(1)} copy(f32[8,128,4,1024]{3,2,1,0:T(4,128)} %all-gather.5.cloned.1.call-done) | data formatting | bytes 33554432 | tf_op jit(solution)/shard_map/all_gather | solution.py:58
  272.0 0.0 copy-done.1
  272.0 0.0 copy-start
  272.0 54.8 %convolution_bitcast_fusion.1 = f32[64,8,8,128]{3,1,2,0:T(8,128)S(1)} fusion(f32[4,1024,512]{2,1,0:T(8,128)S(1)} %copy-done.1, f32[1024,4,1024]{2,0,1:T(8,128)S(1)} %bitcast.29), kind=kOutput, calls=%fused_computation.2 | convolution fusion | flops 25769803776 | bytes 27262976 | tf_op jit(solution)/shard_map/kcl,cln->kn/dot_general | solution.py:61
  326.9 0.5 copy.16
  327.3 0.0 copy-start.2
  327.3 0.3 collective-permute-start
  327.6 1.0 copy-done.2
  328.6 1.4 collective-permute-start.1
  330.0 45.3 %collective-permute-done = f32[8,128,4,128]{1,0,3,2:T(8,128)S(1)} collective-permute-done((f32[8,128,4,128]{1,0,3,2:T(8,128)S(1)}, f32[8,128,4,128]{1,0,3,2:T(8,128)S(1)}, u32[]{:S(2)}, u32[]{:S(2)}) %collective-permute-start) | collective-permute-done | bytes 2097184 | tf_op jit(solution)/shard_map/ppermute | solution.py:16
  375.4 0.0 copy-start.4
  375.4 0.0 collective-permute-start.2
  375.4 0.0 collective-permute-done.1
  375.4 1.3 copy-done.4
  376.7 0.0 copy-start.6
  376.7 1.4 collective-permute-start.3
  378.1 46.1 %collective-permute-done.2 = f32[8,128,4,128]{1,0,3,2:T(8,128)S(1)} collective-permute-done((f32[8,128,4,128]{1,0,3,2:T(8,128)S(1)}, f32[8,128,4,128]{1,0,3,2:T(8,128)S(1)}, u32[]{:S(2)}, u32[]{:S(2)}) %collective-permute-start.2) | collective-permute-done | bytes 2097184 | tf_op jit(solution)/shard_map/ppermute | solution.py:16
  424.2 0.0 copy-done.6
  424.2 0.0 copy-start.8
  424.2 0.0 collective-permute-start.4
  424.2 0.0 collective-permute-done.3
  424.2 1.4 copy-done.8
  425.5 1.3 collective-permute-start.5
  426.8 45.7 %collective-permute-done.4 = f32[8,128,4,128]{1,0,3,2:T(8,128)} collective-permute-done((f32[8,128,4,128]{1,0,3,2:T(8,128)S(1)}, f32[8,128,4,128]{1,0,3,2:T(8,128)}, u32[]{:S(2)}, u32[]{:S(2)}) %collective-permute-start.4) | collective-permute-done | bytes 2097184 | tf_op jit(solution)/shard_map/ppermute | solution.py:16
  472.5 0.0 collective-permute-start.6
  472.5 0.0 copy-done
  472.5 1.8 reshape.37
  474.3 6.8 broadcast_in_dim.4
  481.1 0.0 copy-done.3
  481.1 1.4 constant_dynamic-update-slice_fusion.7
  482.6 0.0 copy-done.5
  482.6 1.5 constant_dynamic-update-slice_fusion.6
  484.1 0.0 copy-done.7
  484.1 1.4 constant_dynamic-update-slice_fusion.5
  485.5 0.0 copy-done.9
  485.5 1.4 constant_dynamic-update-slice_fusion.4
  486.9 3.0 constant_dynamic-update-slice_fusion.3
  489.9 3.0 constant_dynamic-update-slice_fusion.2
  492.9 0.0 collective-permute-done.5
  492.9 3.0 constant_dynamic-update-slice_fusion.1
  496.0 3.2 collective-permute-done.6
  499.1 3.0 constant_dynamic-update-slice_fusion
  502.1 18.2 %reshape.32 = f32[1024,4,1024]{0,2,1:T(8,128)} reshape(f32[8,128,4,1024]{1,0,3,2:T(8,128)} %constant_dynamic-update-slice_fusion) | data formatting | bytes 33554432 | tf_op jit(solution)/shard_map/reshape | solution.py:29
  520.3 0.0 copy-done.10
  520.3 29.1 %convolution_bitcast_fusion = f32[4,8,128,512]{3,2,0,1:T(8,128)S(1)} fusion(f32[8,4,128,1024]{3,2,1,0:T(8,128)} %bitcast.30, f32[1024,512,1,1]{1,0,2,3:T(8,128)S(1)} %copy-done.10), kind=kOutput, calls=%fused_computation | convolution fusion | flops 25769803776 | bytes 27262976 | tf_op jit(solution)/shard_map/kcl,kn->cln/dot_general | solution.py:30
  549.4 4.3 copy.12
  553.6 0.0 reduce-scatter.2.cloned.1.call-update
  553.6 143.9 %reduce-scatter.2.cloned.1.call-done = f32[1024,512]{1,0:T(8,128)} async-done(((f32[4096,512]{1,0:T(8,128)}), f32[1024,512]{1,0:T(8,128)}) %reduce-scatter.2.cloned.1.call-update) | async-done | bytes 2097168 | tf_op jit(solution)/shard_map/reduce_scatter | solution.py:74
  697.5 1.9 reshape.35
  699.5 3.5 add.96
  (6 shorter events, 0.0 us)
Async XLA Ops:
  6.5 157.0 %all-gather.3.cloned.1.call-start = ((), (), s32[]{:S(2)}) async-start(), calls=%async_computation.1 | async-start | bytes 10485760 | tf_op jit(solution)/shard_map/all_gather | solution.py:56
  11.0 245.6 %all-gather.5.cloned.1.call-start = ((), (), s32[]{:S(2)}) async-start(), calls=%async_computation.2 | async-start | bytes 18874368 | tf_op jit(solution)/shard_map/all_gather | solution.py:58
  11.8 685.7 %reduce-scatter.2.cloned.1.call-start = ((), (), s32[]{:S(2)}) async-start(), calls=%async_computation.3 | async-start | bytes 10485760 | tf_op jit(solution)/shard_map/reduce_scatter | solution.py:74
  256.6 15.4 %copy-start.1 = (f32[4,1024,512]{2,1,0:T(8,128)S(1)}, f32[4,1024,512]{2,1,0:T(8,128)}, u32[]{:S(2)}) copy-start(f32[4,1024,512]{2,1,0:T(8,128)} %reshape.29) | copy-start | bytes 25165828
  272.0 200.5 %copy-start = (f32[8,128,4,128]{3,2,1,0:T(4,128)S(1)}, f32[8,128,4,128]{3,2,1,0:T(4,128)}, u32[]{:S(2)}) copy-start(f32[8,128,4,128]{3,2,1,0:T(4,128)} %broadcast_multiply_fusion) | copy-start | bytes 6291460
  327.3 1.3 copy-start.2
  327.3 48.0 %collective-permute-start = (f32[8,128,4,128]{1,0,3,2:T(8,128)S(1)}, f32[8,128,4,128]{1,0,3,2:T(8,128)S(1)}, u32[]{:S(2)}, u32[]{:S(2)}) collective-permute-start(f32[8,128,4,128]{1,0,3,2:T(8,128)S(1)} %bitcast.31), channel_id=1, source_target_pairs={{0,1},{1,2},{2,3},{3,4},{4,5},{5,6},{6,7},{7,0},{8,9},{9,10},{10,1... | collective-permute-start | bytes 6291464 | tf_op jit(solution)/shard_map/ppermute | solution.py:16
  328.6 46.7 %collective-permute-start.1 = (f32[8,128,4,128]{1,0,3,2:T(8,128)S(1)}, f32[8,128,4,128]{1,0,3,2:T(8,128)S(1)}, u32[]{:S(2)}, u32[]{:S(2)}) collective-permute-start(f32[8,128,4,128]{1,0,3,2:T(8,128)S(1)} %bitcast.32), channel_id=1, source_target_pairs={{0,7},{1,0},{2,1},{3,2},{4,3},{5,4},{6,5},{7,6},{8,15},{9,8},{10,9... | collective-permute-start | bytes 6291464 | tf_op jit(solution)/shard_map/ppermute | solution.py:21
  375.4 1.3 copy-start.4
  375.4 48.8 %collective-permute-start.2 = (f32[8,128,4,128]{1,0,3,2:T(8,128)S(1)}, f32[8,128,4,128]{1,0,3,2:T(8,128)S(1)}, u32[]{:S(2)}, u32[]{:S(2)}) collective-permute-start(f32[8,128,4,128]{1,0,3,2:T(8,128)S(1)} %collective-permute-done), channel_id=1, source_target_pairs={{0,1},{1,2},{2,3},{3,4},{4,5},{5,6},{6,7},{7,0},{8,9},{9,10},{10,1... | collective-permute-start | bytes 6291464 | tf_op jit(solution)/shard_map/ppermute | solution.py:16
  376.7 47.5 %copy-start.6 = (f32[8,128,4,128]{1,0,3,2:T(8,128)}, f32[8,128,4,128]{1,0,3,2:T(8,128)S(1)}, u32[]{:S(2)}) copy-start(f32[8,128,4,128]{1,0,3,2:T(8,128)S(1)} %collective-permute-done.1) | copy-start | bytes 6291460
  376.7 47.5 %collective-permute-start.3 = (f32[8,128,4,128]{1,0,3,2:T(8,128)S(1)}, f32[8,128,4,128]{1,0,3,2:T(8,128)}, u32[]{:S(2)}, u32[]{:S(2)}) collective-permute-start(f32[8,128,4,128]{1,0,3,2:T(8,128)S(1)} %collective-permute-done.1), channel_id=1, source_target_pairs={{0,7},{1,0},{2,1},{3,2},{4,3},{5,4},{6,5},{7,6},{8,15},{9,8},{10,9... | collective-permute-start | bytes 6291464 | tf_op jit(solution)/shard_map/ppermute | solution.py:21
  424.2 1.4 copy-start.8
  424.2 48.3 %collective-permute-start.4 = (f32[8,128,4,128]{1,0,3,2:T(8,128)S(1)}, f32[8,128,4,128]{1,0,3,2:T(8,128)}, u32[]{:S(2)}, u32[]{:S(2)}) collective-permute-start(f32[8,128,4,128]{1,0,3,2:T(8,128)S(1)} %collective-permute-done.2), channel_id=1, source_target_pairs={{0,1},{1,2},{2,3},{3,4},{4,5},{5,6},{6,7},{7,0},{8,9},{9,10},{10,1... | collective-permute-start | bytes 6291464 | tf_op jit(solution)/shard_map/ppermute | solution.py:16
  425.5 67.4 %collective-permute-start.5 = (f32[8,128,4,128]{1,0,3,2:T(8,128)}, f32[8,128,4,128]{1,0,3,2:T(8,128)}, u32[]{:S(2)}, u32[]{:S(2)}) collective-permute-start(f32[8,128,4,128]{1,0,3,2:T(8,128)} %collective-permute-done.3), channel_id=1, source_target_pairs={{0,7},{1,0},{2,1},{3,2},{4,3},{5,4},{6,5},{7,6},{8,15},{9,8},{10,9... | collective-permute-start | bytes 6291464 | tf_op jit(solution)/shard_map/ppermute | solution.py:21
  472.5 26.7 %collective-permute-start.6 = (f32[8,128,4,128]{1,0,3,2:T(8,128)}, f32[8,128,4,128]{1,0,3,2:T(8,128)}, u32[]{:S(2)}, u32[]{:S(2)}) collective-permute-start(f32[8,128,4,128]{1,0,3,2:T(8,128)} %collective-permute-done.4), channel_id=1, source_target_pairs={{0,1},{1,2},{2,3},{3,4},{4,5},{5,6},{6,7},{7,0},{8,9},{9,10},{10,1... | collective-permute-start | bytes 6291464 | tf_op jit(solution)/shard_map/ppermute | solution.py:16
  474.3 6.8 copy-start.3
  474.3 8.3 %copy-start.5 = (f32[8,128,4,128]{1,0,3,2:T(8,128)S(1)}, f32[8,128,4,128]{1,0,3,2:T(8,128)}, u32[]{:S(2)}) copy-start(f32[8,128,4,128]{1,0,3,2:T(8,128)} %copy-done.4) | copy-start | bytes 6291460
  481.1 2.9 copy-start.7
  481.1 4.4 copy-start.9
  502.1 18.2 %copy-start.10 = (f32[1024,512,1,1]{1,0,2,3:T(8,128)S(1)}, f32[1024,512,1,1]{1,0,2,3:T(8,128)}, u32[]{:S(2)}) copy-start(f32[1024,512,1,1]{1,0,2,3:T(8,128)} %reshape.37) | copy-start | bytes 6291460
Sparse Core Ops, SparseCore 0:
  11.1 152.3 all-gather.2
  165.4 91.1 all-gather.4
  553.8 143.7 reduce-scatter.1
